TPU v7x, 32 devices: a whole 2x2x4 slice. The times are simulated.
32 devices in a mesh: grp: 4 (over y, core), head: 8 (over z, x).
Axes of the slice: x: 2, y: 2, z: 4, core: 2. Of those that a mesh axis runs over, the one named last changes fastest.
Arguments:
- hidden_in: bfloat16 [96, 4096], P('grp', 'head'), may hold values from -6 to 6
- attention_gain: float32 [4096], replicated, may hold values from 0.1 to 1.9
- w_query: bfloat16 [4096, 4096], P(None, 'head'), may hold values from -0.09375 to 0.09375
- w_key_value: bfloat16 [2, 4096, 4096], P(None, None, 'head'), as said below
- w_attention_out: bfloat16 [4096, 4096], P('head'), may hold values from -0.09375 to 0.09375
- past_cache: bfloat16 [2, 96, 32, 128, 128], P(None, 'grp', 'head'), may hold values from -2000 to 2000, as said below
- lengths: int32 [96], P('grp'), may hold values from 2 to 128, as said below
- mamba_gain: float32 [4096], replicated, may hold values from 0.1 to 1.9
- w_in: bfloat16 [2, 4096, 8192], P(None, None, 'head'), may hold values from -0.09375 to 0.09375
- filter_weight: float32 [4, 8192], P(None, 'head'), may hold values from -3 to 3
- filter_bias: float32 [8192], P('head'), may hold values from -1.8 to 1.8
- filter_state: float32 [96, 3, 8192], P('grp', None, 'head'), may hold values from -6 to 6
- w_select: bfloat16 [8192, 288], P('head'), may hold values from -0.0625 to 0.0625
- w_step: bfloat16 [256, 8192], P(None, 'head'), may hold values from -0.375 to 0.375
- step_bias: float32 [8192], P('head'), may hold values from -4 to -1
- log_rate: float32 [16, 8192], P(None, 'head'), may hold values from 0 to 2.77
- skip_gain: float32 [8192], P('head'), may hold values from 0.1 to 1.9
- scan_state: float32 [96, 16, 8192], P('grp', None, 'head'), may hold values from -6 to 6
- w_mamba_out: bfloat16 [8192, 4096], P('head'), may hold values from -0.0625 to 0.0625
- reward_terms: float32 [96, 128], P('grp', 'head'), may hold values from -60 to 60
- reward_mask: int32 [96, 128], P('grp', 'head'), may hold values 0 or 1
Outputs:
- hidden_out: bfloat16 [96, 4096], P('grp', 'head')
- new_key_value: bfloat16 [2, 96, 32, 128], P(None, 'grp', 'head')
- new_filter_state: float32 [96, 3, 8192], P('grp', None, 'head')
- new_scan_state: float32 [96, 16, 8192], P('grp', None, 'head')
- rewards: float32 [96], P('grp')
Inputs may be any that keep to these rules, and one draw needn't show every extreme that they name: `w_key_value`: query heads that share a key-value head (4 of them in a row) hold equal copies. `past_cache`: query heads that share a key-value head (4 of them in a row) hold equal copies. `lengths`: the first sample's cache is full (128).
All inputs are finite; a program needn't handle non-finite values. No bound on the sum of `reward_mask` on one device may be relied on, other than what follows from the above.
Results may differ from a plain program's by a relative error of at most 0.012.
Values may be sent and summed in bfloat16 or wider, within the bound.
No kernel may reach another device: no remote copies, remote signals or barrier semaphores. Data moves between devices by JAX's collectives and lax.ppermute only.
A program may use at most 128 MiB of HBM per device.

v0:
```python
import math

import jax
import jax.numpy as jnp
from jax import lax
from jax.sharding import PartitionSpec as P

EPS = 1e-06


def norm_rows(row_values, gain):
    values = row_values.astype(jnp.float32)
    factor = lax.rsqrt(jnp.mean(values * values, axis=-1, keepdims=True) + EPS)
    return (values * factor * gain).astype(jnp.bfloat16)


def attend_block(queries, past_cache, fresh, lengths):
    inv_root = 1.0 / math.sqrt(queries.shape[-1])
    scores = (
        jnp.einsum("bhd,bhtd->bht", queries, past_cache[0], preferred_element_type=jnp.float32)
        * inv_root
    )
    positions = lax.iota(jnp.int32, past_cache.shape[3])
    scores = jnp.where(positions[None, None, :] < lengths[:, None, None], scores, -jnp.inf)
    own_score = (
        jnp.einsum("bhd,bhd->bh", queries, fresh[0], preferred_element_type=jnp.float32) * inv_root
    )
    row_max = jnp.maximum(jnp.max(scores, axis=-1), own_score)
    weights = jnp.exp(scores - row_max[:, :, None])
    own_weight = jnp.exp(own_score - row_max)
    denominator = jnp.sum(weights, axis=-1) + own_weight
    weights = (weights / denominator[:, :, None]).astype(jnp.bfloat16)
    own_weight = (own_weight / denominator).astype(jnp.bfloat16)
    blended = jnp.einsum(
        "bht,bhtd->bhd", weights, past_cache[1], preferred_element_type=jnp.float32
    )
    blended = blended + own_weight.astype(jnp.float32)[:, :, None] * fresh[1].astype(jnp.float32)
    return blended.astype(jnp.bfloat16)


def reward_partial(reward_terms, reward_mask, lengths):
    columns = reward_terms.shape[1]
    positions = lax.axis_index("head") * columns + lax.iota(jnp.int32, columns)
    live = (reward_mask == 1) & (positions[None, :] < lengths[:, None])
    return jnp.sum(jnp.where(live, reward_terms, 0.0), axis=1)


def local(
    hidden_in,
    attention_gain,
    w_query,
    w_key_value,
    w_attention_out,
    past_cache,
    lengths,
    mamba_gain,
    w_in,
    filter_weight,
    filter_bias,
    filter_state,
    w_select,
    w_step,
    step_bias,
    log_rate,
    skip_gain,
    scan_state,
    w_mamba_out,
    reward_terms,
    reward_mask,
):
    samples = hidden_in.shape[0]
    shard_width = hidden_in.shape[1]
    local_heads = past_cache.shape[2]
    head_size = past_cache.shape[4]
    rank_width = w_step.shape[0]
    state_width = log_rate.shape[0]
    rewards = lax.psum(reward_partial(reward_terms, reward_mask, lengths), "head")
    full_in = lax.all_gather(hidden_in, "head", axis=1, tiled=True)
    normed = norm_rows(full_in, attention_gain)
    queries = jnp.dot(normed, w_query, preferred_element_type=jnp.float32).astype(jnp.bfloat16)
    queries = queries.reshape(samples, local_heads, head_size)
    fresh_all = jnp.einsum("bd,kdc->kbc", normed, w_key_value, preferred_element_type=jnp.float32)
    new_key_value = fresh_all.astype(jnp.bfloat16).reshape(2, samples, local_heads, head_size)
    attended = attend_block(queries, past_cache, new_key_value, lengths)
    attended = attended.reshape(samples, local_heads * head_size)
    head_terms = jnp.dot(attended, w_attention_out, preferred_element_type=jnp.float32)
    summed = lax.psum(head_terms, "head")
    mixed_full = (full_in.astype(jnp.float32) + summed).astype(jnp.bfloat16)
    mixed = lax.dynamic_slice_in_dim(
        mixed_full, lax.axis_index("head") * shard_width, shard_width, 1
    )
    normed_two = norm_rows(mixed_full, mamba_gain)
    x_inner = jnp.dot(normed_two, w_in[0], preferred_element_type=jnp.float32)
    gate_part = jnp.dot(normed_two, w_in[1], preferred_element_type=jnp.float32)
    taps = filter_weight.shape[0]
    conv_sum = filter_bias + x_inner * filter_weight[taps - 1]
    for tap_index in range(taps - 1):
        conv_sum = conv_sum + filter_state[:, tap_index, :] * filter_weight[tap_index]
    conv_out = jax.nn.silu(conv_sum).astype(jnp.bfloat16)
    new_filter_state = jnp.concatenate([filter_state[:, 1:, :], x_inner[:, None, :]], axis=1)
    local_select = jnp.dot(conv_out, w_select, preferred_element_type=jnp.float32)
    projected = lax.psum(local_select, "head")
    step_low = projected[:, :rank_width].astype(jnp.bfloat16)
    b_input = projected[:, rank_width : rank_width + state_width]
    c_output = projected[:, rank_width + state_width :]
    step_size = jax.nn.softplus(
        jnp.dot(step_low, w_step, preferred_element_type=jnp.float32) + step_bias
    )
    conv_value = conv_out.astype(jnp.float32)
    decay_rate = jnp.exp(-step_size[:, None, :] * jnp.exp(log_rate)[None, :, :])
    new_scan_state = (
        decay_rate * scan_state
        + step_size[:, None, :] * b_input[:, :, None] * conv_value[:, None, :]
    )
    scan_out = (
        jnp.sum(c_output[:, :, None] * new_scan_state, axis=1) + skip_gain * conv_value
    ) * jax.nn.silu(gate_part)
    scan_out = scan_out.astype(jnp.bfloat16)
    channel_terms = jnp.dot(scan_out, w_mamba_out, preferred_element_type=jnp.float32)
    mamba_sum = lax.psum_scatter(channel_terms, "head", scatter_dimension=1, tiled=True)
    hidden_out = (mixed.astype(jnp.float32) + mamba_sum).astype(jnp.bfloat16)
    return (hidden_out, new_key_value, new_filter_state, new_scan_state, rewards)


def solution(mesh):
    placed = (
        P("grp", "head"),
        P(),
        P(None, "head"),
        P(None, None, "head"),
        P("head", None),
        P(None, "grp", "head", None, None),
        P("grp"),
        P(),
        P(None, None, "head"),
        P(None, "head"),
        P("head"),
        P("grp", None, "head"),
        P("head", None),
        P(None, "head"),
        P("head"),
        P(None, "head"),
        P("head"),
        P("grp", None, "head"),
        P("head", None),
        P("grp", "head"),
        P("grp", "head"),
    )
    return jax.shard_map(
        local,
        mesh=mesh,
        in_specs=placed,
        out_specs=(
            P("grp", "head"),
            P(None, "grp", "head", None),
            P("grp", None, "head"),
            P("grp", None, "head"),
            P("grp"),
        ),
        check_vma=False,
    )
```

profile of v0, /device:TPU:0, one launch (start us, length us, event | category | flops | bytes accessed | tf_op | source)
XLA Modules:
  0.0 255.5 jit_solution(5977101583924743962)
XLA Ops:
  7.2 0.0 all-reduce.3.cloned.1.call-start
  7.2 32.8 %all_gather.3 = bf16[24,4096]{1,0:T(8,128)(2,1)S(1)} all-gather(bf16[24,512]{1,0:T(8,128)(2,1)} %param.21), channel_id=1, replica_groups=mesh['grp'=4,'head'=8] {'head'}, dimensions={1}, use_global_device_ids=true | all-gather | bytes 221184 | tf_op jit(solution)/shard_map/all_gather | solution.py:78
  40.0 0.2 fusion.16
  40.2 2.9 %convolution_convert_fusion.1 = bf16[24,512]{1,0:T(8,128)(2,1)S(1)} fusion(bf16[4096,512]{1,0:T(8,128)(2,1)} %param.23, bf16[24,4096]{1,0:T(8,128)(2,1)S(1)} %all_gather.3, f32[4096]{0:T(1024)} %param.22, f32[24]{0:T(128)S(1)} %add_rsqrt_fusion.1), kind=kOutput, calls=%fused_computation.17 | convolution fusion | flops 101068800 | bytes 4431968 | tf_op jit(solution)/shard_map/dot_general | solution.py:80
  43.2 4.6 %fusion.12 = bf16[2,24,512]{2,1,0:T(8,128)(2,1)S(1)} fusion(bf16[2,4096,512]{2,1,0:T(8,128)(2,1)} %param.24, bf16[24,4096]{1,0:T(8,128)(2,1)S(1)} %all_gather.3, f32[4096]{0:T(1024)S(1)} %copy-done.4, f32[24]{0:T(128)S(1)} %add_rsqrt_fusion.1), kind=kOutput, calls=%fused_computation.16 | convolution fusion | flops 201744384 | bytes 8650848 | tf_op jit(solution)/shard_map/bd,kdc->kbc/dot_general | solution.py:82
  47.9 0.1 fusion.31
  48.0 0.1 copy.32
  48.1 0.1 iota_compare_fusion
  48.1 3.6 %fusion.8 = f32[24,4,1,128]{3,2,1,0:T(1,128)S(1)} fusion(bf16[24,4,128,1]{2,3,1,0:T(2,128)(2,1)S(1)} %reshape.94, bf16[2,24,4,128,128]{4,3,2,1,0:T(8,128)(2,1)} %param.26), kind=kOutput, calls=%fused_computation.8 | convolution fusion | flops 3145728 | bytes 3219456 | tf_op jit(solution)/shard_map/bhd,bhtd->bht/dot_general | solution.py:20
  51.8 0.1 fusion.42
  51.8 0.2 fusion.41
  52.0 0.1 fusion.47
  52.2 2.9 %fusion.6 = f32[24,4,1,128]{3,2,1,0:T(1,128)S(1)} fusion(bf16[2,24,4,128,128]{4,3,2,1,0:T(8,128)(2,1)} %param.26, bf16[24,4,128,1]{2,0,1,3:T(8,128)(2,1)S(1)} %fusion.47), kind=kOutput, calls=%fused_computation.6 | convolution fusion | flops 3145728 | bytes 3219456 | tf_op jit(solution)/shard_map/bht,bhtd->bhd/dot_general | solution.py:34
  55.1 0.1 copy.26
  55.2 0.1 add_convert_fusion.1
  55.3 3.6 %fusion.43 = f32[24,4096]{1,0:T(8,128)} fusion(bf16[512,4096]{1,0:T(8,128)(2,1)} %param.25, bf16[3,8,4,128]{3,2,1,0:T(4,128)(2,1)S(1)} %bitcast.81), kind=kOutput, calls=%fused_computation.57 | convolution fusion | flops 100663296 | bytes 4612096 | tf_op jit(solution)/shard_map/dot_general | solution.py:86
  58.9 0.0 all-reduce.3.cloned.1.call-update
  58.9 0.0 reduce-scatter.2.cloned.1.call-start
  59.1 0.1 select_reduce_fusion
  59.2 72.6 %all-reduce.3.cloned.1.call-done = f32[24,4096]{1,0:T(8,128)} async-done(((f32[24,4096]{1,0:T(8,128)}), f32[24,4096]{1,0:T(8,128)}) %all-reduce.3.cloned.1.call-update) | async-done | bytes 393232 | tf_op jit(solution)/shard_map/psum | solution.py:87
  131.8 1.2 fusion.13
  133.1 5.5 %fusion.51 = (f32[24,1024]{1,0:T(8,128)}, bf16[24,1024]{1,0:T(8,128)(2,1)S(1)}, f32[24,1024]{1,0:T(8,128)S(1)}) fusion(f32[1024]{0:T(1024)S(1)} %bitcast.86, f32[24,3,1024]{2,0,1:T(8,128)S(1)} %copy-done.2, f32[1024]{0:T(1024)S(1)} %bitcast.87, f32[1024]{0:T(1024)S(1)} %bitcast.85, f32[1024]{0:T(1024)S(1)} %bitcast.84, f32[1024]{0:T(1024)S(1)} %copy-done.13, ...), kind=kOutput, calls=%fused_computation.75 | convolution fusion | flops 202063872 | bytes 9162848 | tf_op jit(solution)/shard_map/dot_general | solution.py:93
  138.5 0.3 fusion.56
  138.8 36.1 %all-reduce = (f32[24,288]{1,0:T(8,128)S(1)}, f32[24]{0:T(128)}) all-reduce(f32[24,288]{1,0:T(8,128)S(1)} %fusion.56, f32[24]{0:T(128)S(1)} %select_reduce_fusion), channel_id=1, replica_groups=mesh['grp'=4,'head'=8] {'head'}, use_global_device_ids=true, to_apply=%region_5.6 | all-reduce | flops 6936 | bytes 55488 | tf_op jit(solution)/shard_map/psum | solution.py:102
  174.9 0.1 fusion.53
  175.0 0.2 fusion.55
  175.2 2.8 %multiply_reduce_fusion = (f32[24,1024]{1,0:T(8,128)S(1)}, f32[24,16,1024]{2,1,0:T(8,128)}) fusion(f32[24,16]{1,0:T(8,128)S(1)} %get-tuple-element.16, f32[24,1024]{1,0:T(8,128)} %get-tuple-element.9, f32[24,16]{1,0:T(8,128)S(1)} %get-tuple-element.15, f32[24,1024]{1,0:T(8,128)S(1)} %get-tuple-element.25, f32[24,16,1024]{2,1,0:T(8,128)S(1)} %copy-done.1, ...), kind=kLoop, calls=%fused_computation.12 | loop fusion | flops 2727936 | bytes 3607552 | tf_op jit(solution)/shard_map/reduce_sum | solution.py:116
  178.1 8.9 %fusion.27 = f32[24,4096]{1,0:T(8,128)} fusion(bf16[1024,4096]{1,0:T(8,128)(2,1)} %param.39, bf16[2,4096,1024]{2,1,0:T(8,128)(2,1)} %param.29, f32[24,1024]{1,0:T(8,128)S(1)} %get-tuple-element.7, f32[1024]{0:T(1024)S(1)} %copy-done.11, bf16[24,4096]{1,0:T(8,128)(2,1)S(1)} %get-tuple-element.12, f32[4096]{0:T(1024)S(1)} %copy-done.7, ...), kind=kOutput, calls=%fused_computation.40 | convolution fusion | flops 403267584 | bytes 17535072 | tf_op jit(solution)/shard_map/dot_general | solution.py:119
  187.0 0.6 reshape.84
  187.7 0.7 pad_maximum_fusion
  188.4 58.9 %reduce-scatter.2.cloned.1.call-done = f32[24,512]{1,0:T(8,128)} async-done(((f32[24,4096]{1,0:T(8,128)}), f32[24,512]{1,0:T(8,128)}) %reduce-scatter.2.cloned.1.call-update) | async-done | bytes 49168 | tf_op jit(solution)/shard_map/reduce_scatter | solution.py:120
  247.3 1.4 add_convert_fusion
  (43 shorter events, 0.3 us)
Async XLA Ops:
  7.2 131.4 %copy-start = (bf16[1024,288]{0,1:T(8,128)(2,1)S(1)}, bf16[1024,288]{0,1:T(8,128)(2,1)}, u32[]{:S(2)}) copy-start(bf16[1024,288]{0,1:T(8,128)(2,1)} %param.33) | copy-start | bytes 1769476
  7.2 36.0 %copy-start.4 = (f32[4096]{0:T(1024)S(1)}, f32[4096]{0:T(1024)}, u32[]{:S(2)}) copy-start(f32[4096]{0:T(1024)} %param.22) | copy-start | bytes 49156
  7.2 124.6 %all-reduce.3.cloned.1.call-start = ((), (), s32[]{:S(2)}) async-start(), calls=%async_computation.1 | async-start | bytes 786432 | tf_op jit(solution)/shard_map/psum | solution.py:87
  43.2 4.9 %copy-start.12 = (s32[24]{0:T(128)S(1)}, s32[24]{0:T(128)}, u32[]{:S(2)}) copy-start(s32[24]{0:T(128)} %param.27) | copy-start | bytes 292
  52.2 6.8 %copy-start.5 = (f32[16,1024]{1,0:T(8,128)S(1)}, f32[16,1024]{1,0:T(8,128)}, u32[]{:S(2)}) copy-start(f32[16,1024]{1,0:T(8,128)} %param.36) | copy-start | bytes 196612
  52.2 6.9 %copy-start.8 = (f32[24,16]{0,1:T(8,128)S(1)}, f32[24,16]{0,1:T(8,128)}, u32[]{:S(2)}) copy-start(f32[24,16]{0,1:T(8,128)} %param.40) | copy-start | bytes 4612
  52.2 6.9 %copy-start.9 = (s32[24,16]{0,1:T(8,128)S(1)}, s32[24,16]{0,1:T(8,128)}, u32[]{:S(2)}) copy-start(s32[24,16]{0,1:T(8,128)} %param.41) | copy-start | bytes 4612
  52.2 7.0 %copy-start.6 = (f32[4,1024]{1,0:T(4,128)S(1)}, f32[4,1024]{1,0:T(4,128)}, u32[]{:S(2)}) copy-start(f32[4,1024]{1,0:T(4,128)} %param.30) | copy-start | bytes 49156
  52.2 80.8 %copy-start.2 = (f32[24,3,1024]{2,0,1:T(8,128)S(1)}, f32[24,3,1024]{2,0,1:T(8,128)}, u32[]{:S(2)}) copy-start(f32[24,3,1024]{2,0,1:T(8,128)} %param.32) | copy-start | bytes 884740
  52.2 80.8 %copy-start.7 = (f32[4096]{0:T(1024)S(1)}, f32[4096]{0:T(1024)}, u32[]{:S(2)}) copy-start(f32[4096]{0:T(1024)} %param.28) | copy-start | bytes 49156
  52.2 80.8 %copy-start.13 = (f32[1024]{0:T(1024)S(1)}, f32[1024]{0:T(1024)}, u32[]{:S(2)}) copy-start(f32[1024]{0:T(1024)} %param.31) | copy-start | bytes 12292
  58.9 188.3 %reduce-scatter.2.cloned.1.call-start = ((), (), s32[]{:S(2)}) async-start(), calls=%async_computation.2 | async-start | bytes 442368 | tf_op jit(solution)/shard_map/reduce_scatter | solution.py:120
  133.0 41.9 %copy-start.3 = (bf16[256,1024]{1,0:T(8,128)(2,1)S(1)}, bf16[256,1024]{1,0:T(8,128)(2,1)}, u32[]{:S(2)}) copy-start(bf16[256,1024]{1,0:T(8,128)(2,1)} %param.34) | copy-start | bytes 1572868
  133.0 41.9 %copy-start.10 = (f32[1024]{0:T(1024)S(1)}, f32[1024]{0:T(1024)}, u32[]{:S(2)}) copy-start(f32[1024]{0:T(1024)} %param.35) | copy-start | bytes 12292
  133.0 42.2 %copy-start.1 = (f32[24,16,1024]{2,1,0:T(8,128)S(1)}, f32[24,16,1024]{2,1,0:T(8,128)}, u32[]{:S(2)}) copy-start(f32[24,16,1024]{2,1,0:T(8,128)} %param.38) | copy-start | bytes 4718596
  138.5 39.5 %copy-start.11 = (f32[1024]{0:T(1024)S(1)}, f32[1024]{0:T(1024)}, u32[]{:S(2)}) copy-start(f32[1024]{0:T(1024)} %param.37) | copy-start | bytes 12292
  178.1 9.6 %slice-start = ((f32[24,3,1024]{2,0,1:T(8,128)}), f32[24,2,1024]{2,0,1:T(8,128)S(1)}, s32[]{:S(2)}) async-start(f32[24,3,1024]{2,0,1:T(8,128)} %param.32), calls=%async_computation.3 | async-start | bytes 393216 | tf_op jit(solution)/shard_map/slice | solution.py:100
Sparse Core Ops, SparseCore 0:
  59.1 72.7 all-reduce.2
  187.2 60.0 reduce-scatter.1
where the time goes:
time: 256 us
  waiting for transfers between devices  132 us (52%)
  blocking collectives  68.9 us (27%)
  matrix products  32.5 us (13%)
  between operations  14.3 us (6%)
  other arithmetic  7.1 us (3%)
    psum x1, waiting for transfers between devices, local(): summed = lax.psum(head_terms, 'head')  72.6 us
    reduce_scatter x1, waiting for transfers between devices, local(): lax.psum_scatter(channel_terms, 'head', scatter_dimension=1, tiled=True)  58.9 us
    psum x1, blocking collectives, local(): projected = lax.psum(local_select, 'head')  36.1 us
    all_gather x1, blocking collectives, local(): full_in = lax.all_gather(hidden_in, 'head', axis=1, tiled=True)  32.8 us
    dot_general x1, matrix products, local(): jnp.dot(scan_out, w_mamba_out, preferred_element_type=jnp.float32)  8.95 us
    dot_general x1, matrix products, local(): x_inner = jnp.dot(normed_two, w_in[0], preferred_element_type=jnp.float32)  5.46 us
  transfers between devices with their start and end apart: 2, of which 2 were waited for; matrix products, arithmetic and copies ran while one was open for 1% of the time, Pallas kernels for 0%

commit v1 on v0

--- a/solution.py
+++ b/solution.py
@@ -14,27 +14,65 @@
     return (values * factor * gain).astype(jnp.bfloat16)
 
 
-def attend_block(queries, past_cache, fresh, lengths):
+SHARED = 4
+
+
+def exchange(parts):
+    return lax.all_to_all(parts, "head", 0, 0)
+
+
+def spread(block):
+    peers = lax.axis_size("head")
+    return exchange(jnp.broadcast_to(block[None], (peers,) + block.shape))
+
+
+def add_scattered(terms):
+    peers = lax.axis_size("head")
+    rows, width = terms.shape
+    parts = terms.astype(jnp.bfloat16).reshape(rows, peers, width // peers)
+    received = exchange(jnp.transpose(parts, (1, 0, 2)))
+    return jnp.sum(received.astype(jnp.float32), axis=0)
+
+
+def side_by_side(blocks):
+    peers, rows, width = blocks.shape
+    return jnp.transpose(blocks, (1, 0, 2)).reshape(rows, peers * width)
+
+
+def split_float(value):
+    high = value.astype(jnp.bfloat16)
+    rest = value - high.astype(jnp.float32)
+    middle = rest.astype(jnp.bfloat16)
+    low = (rest - middle.astype(jnp.float32)).astype(jnp.bfloat16)
+    return jnp.stack([high, middle, low], axis=1)
+
+
+def attend_block(queries, keys, values, fresh, lengths):
     inv_root = 1.0 / math.sqrt(queries.shape[-1])
     scores = (
-        jnp.einsum("bhd,bhtd->bht", queries, past_cache[0], preferred_element_type=jnp.float32)
+        jnp.einsum("bgqd,bgtd->bgqt", queries, keys, preferred_element_type=jnp.float32) * inv_root
+    )
+    positions = lax.iota(jnp.int32, keys.shape[2])
+    live = positions[None, None, None, :] < lengths[:, None, None, None]
+    scores = jnp.where(live, scores, -jnp.inf)
+    own_score = (
+        jnp.sum(
+            queries.astype(jnp.float32) * fresh[0].astype(jnp.float32)[:, :, None, :], axis=-1
+        )
         * inv_root
     )
-    positions = lax.iota(jnp.int32, past_cache.shape[3])
-    scores = jnp.where(positions[None, None, :] < lengths[:, None, None], scores, -jnp.inf)
-    own_score = (
-        jnp.einsum("bhd,bhd->bh", queries, fresh[0], preferred_element_type=jnp.float32) * inv_root
-    )
     row_max = jnp.maximum(jnp.max(scores, axis=-1), own_score)
-    weights = jnp.exp(scores - row_max[:, :, None])
+    weights = jnp.exp(scores - row_max[..., None])
     own_weight = jnp.exp(own_score - row_max)
     denominator = jnp.sum(weights, axis=-1) + own_weight
-    weights = (weights / denominator[:, :, None]).astype(jnp.bfloat16)
+    weights = (weights / denominator[..., None]).astype(jnp.bfloat16)
     own_weight = (own_weight / denominator).astype(jnp.bfloat16)
-    blended = jnp.einsum(
-        "bht,bhtd->bhd", weights, past_cache[1], preferred_element_type=jnp.float32
-    )
-    blended = blended + own_weight.astype(jnp.float32)[:, :, None] * fresh[1].astype(jnp.float32)
+    blended = jnp.einsum("bgqt,bgtd->bgqd", weights, values, preferred_element_type=jnp.float32)
+    blended = (
+        blended
+        + own_weight.astype(jnp.float32)[..., None]
+        * fresh[1].astype(jnp.float32)[:, :, None, :]
+    )
     return blended.astype(jnp.bfloat16)
 
 
@@ -69,29 +107,43 @@
     reward_mask,
 ):
     samples = hidden_in.shape[0]
-    shard_width = hidden_in.shape[1]
     local_heads = past_cache.shape[2]
     head_size = past_cache.shape[4]
     rank_width = w_step.shape[0]
     state_width = log_rate.shape[0]
-    rewards = lax.psum(reward_partial(reward_terms, reward_mask, lengths), "head")
-    full_in = lax.all_gather(hidden_in, "head", axis=1, tiled=True)
+    copies = math.gcd(SHARED, local_heads)
+    kv_heads = local_heads // copies
+    peers = lax.axis_size("head")
+    full_in = side_by_side(spread(hidden_in))
     normed = norm_rows(full_in, attention_gain)
     queries = jnp.dot(normed, w_query, preferred_element_type=jnp.float32).astype(jnp.bfloat16)
-    queries = queries.reshape(samples, local_heads, head_size)
-    fresh_all = jnp.einsum("bd,kdc->kbc", normed, w_key_value, preferred_element_type=jnp.float32)
-    new_key_value = fresh_all.astype(jnp.bfloat16).reshape(2, samples, local_heads, head_size)
-    attended = attend_block(queries, past_cache, new_key_value, lengths)
+    queries = queries.reshape(samples, kv_heads, copies, head_size)
+    group_width = copies * head_size
+    w_single = jnp.concatenate(
+        [
+            w_key_value[:, :, group * group_width : group * group_width + head_size]
+            for group in range(kv_heads)
+        ],
+        axis=2,
+    )
+    fresh_all = jnp.stack(
+        [jnp.dot(normed, w_single[side], preferred_element_type=jnp.float32) for side in range(2)]
+    )
+    fresh = fresh_all.astype(jnp.bfloat16).reshape(2, samples, kv_heads, head_size)
+    new_key_value = jnp.broadcast_to(
+        fresh[:, :, :, None, :], (2, samples, kv_heads, copies, head_size)
+    ).reshape(2, samples, local_heads, head_size)
+    keys = past_cache[0, :, ::copies]
+    values = past_cache[1, :, ::copies]
+    attended = attend_block(queries, keys, values, fresh, lengths)
     attended = attended.reshape(samples, local_heads * head_size)
     head_terms = jnp.dot(attended, w_attention_out, preferred_element_type=jnp.float32)
-    summed = lax.psum(head_terms, "head")
-    mixed_full = (full_in.astype(jnp.float32) + summed).astype(jnp.bfloat16)
-    mixed = lax.dynamic_slice_in_dim(
-        mixed_full, lax.axis_index("head") * shard_width, shard_width, 1
-    )
+    mixed = (hidden_in.astype(jnp.float32) + add_scattered(head_terms)).astype(jnp.bfloat16)
+    mixed_full = side_by_side(spread(mixed))
     normed_two = norm_rows(mixed_full, mamba_gain)
     x_inner = jnp.dot(normed_two, w_in[0], preferred_element_type=jnp.float32)
-    gate_part = jnp.dot(normed_two, w_in[1], preferred_element_type=jnp.float32)
+    gate = jax.nn.silu(jnp.dot(normed_two, w_in[1], preferred_element_type=jnp.float32))
+    gate = lax.optimization_barrier(gate)
     taps = filter_weight.shape[0]
     conv_sum = filter_bias + x_inner * filter_weight[taps - 1]
     for tap_index in range(taps - 1):
@@ -99,7 +151,12 @@
     conv_out = jax.nn.silu(conv_sum).astype(jnp.bfloat16)
     new_filter_state = jnp.concatenate([filter_state[:, 1:, :], x_inner[:, None, :]], axis=1)
     local_select = jnp.dot(conv_out, w_select, preferred_element_type=jnp.float32)
-    projected = lax.psum(local_select, "head")
+    reward_columns = split_float(reward_partial(reward_terms, reward_mask, lengths))
+    sent = jnp.concatenate([local_select.astype(jnp.bfloat16), reward_columns], axis=1)
+    totals = jnp.sum(spread(sent).astype(jnp.float32), axis=0)
+    select_width = w_select.shape[1]
+    projected = totals[:, :select_width]
+    rewards = jnp.sum(totals[:, select_width:], axis=1)
     step_low = projected[:, :rank_width].astype(jnp.bfloat16)
     b_input = projected[:, rank_width : rank_width + state_width]
     c_output = projected[:, rank_width + state_width :]
@@ -114,10 +171,10 @@
     )
     scan_out = (
         jnp.sum(c_output[:, :, None] * new_scan_state, axis=1) + skip_gain * conv_value
-    ) * jax.nn.silu(gate_part)
+    ) * gate
     scan_out = scan_out.astype(jnp.bfloat16)
     channel_terms = jnp.dot(scan_out, w_mamba_out, preferred_element_type=jnp.float32)
-    mamba_sum = lax.psum_scatter(channel_terms, "head", scatter_dimension=1, tiled=True)
+    mamba_sum = add_scattered(channel_terms)
     hidden_out = (mixed.astype(jnp.float32) + mamba_sum).astype(jnp.bfloat16)
     return (hidden_out, new_key_value, new_filter_state, new_scan_state, rewards)
 

time: 256 us -> 89.6 us (0.35)
  waiting for transfers between devices: 132 us -> 30.3 us
  blocking collectives: 68.9 us -> 0 us
  starting transfers between devices: 0.08 us -> 20.8 us
  between operations: 14.3 us -> 1.05 us
  matrix products: 32.5 us -> 24.5 us
  local copies, waits for them, and re-layouts: 1.08 us -> 6.21 us
    psum x1 -> x0, waiting for transfers between devices: 72.6 us -> none  [local(): summed = lax.psum(head_terms, 'head')]
    reduce_scatter x1 -> x0, waiting for transfers between devices: 58.9 us -> none  [local(): lax.psum_scatter(channel_terms, 'head', scatter_dimension=1, tiled=True)]
    psum x1 -> x0, blocking collectives: 36.1 us -> none  [local(): projected = lax.psum(local_select, 'head')]
    all_gather x1 -> x0, blocking collectives: 32.8 us -> none  [local(): full_in = lax.all_gather(hidden_in, 'head', axis=1, tiled=True)]
    all_to_all x0 -> x5, waiting for transfers between devices: none -> 30.3 us  [exchange(): return lax.all_to_all(parts, 'head', 0, 0)]
    all_to_all x0 -> x5, starting transfers between devices: none -> 20.8 us  [exchange(): return lax.all_to_all(parts, 'head', 0, 0)]
    dot_general x1, matrix products: 8.95 us -> 4.63 us  [local(): jnp.dot(scan_out, w_mamba_out, preferred_element_type=jnp.float32)]
    dot_general x1, matrix products: 3.6 us -> 0.66 us  [local(): jnp.dot(attended, w_attention_out, preferred_element_type=jnp.float32)]
  transfers between devices with their start and end apart: 2 -> 5, of which waited for: 2 -> 5; matrix products, arithmetic and copies ran while one was open for 1% -> 9% of each run, Pallas kernels for 0% -> 0%
where the time goes in v1:
time: 89.6 us; the launch traced here: 88.8 us
  waiting for transfers between devices  30.3 us (34%)
  matrix products  24.5 us (27%)
  starting transfers between devices  20.8 us (23%)
  local copies, waits for them, and re-layouts  6.21 us (7%)
  other arithmetic  5.94 us (7%)
  between operations  1.05 us (1%)
    all_to_all x5, waiting for transfers between devices, exchange(): return lax.all_to_all(parts, 'head', 0, 0)  30.3 us
    all_to_all x5, starting transfers between devices, exchange(): return lax.all_to_all(parts, 'head', 0, 0)  20.8 us
    dot_general x1, matrix products, local(): jnp.dot(normed_two, w_in[1], preferred_element_type=jnp.float32)  4.75 us
    dot_general x1, matrix products, local(): jnp.dot(scan_out, w_mamba_out, preferred_element_type=jnp.float32)  4.63 us
    dot_general x1, matrix products, local(): x_inner = jnp.dot(normed_two, w_in[0], preferred_element_type=jnp.float32)  4.62 us
    dot_general x2, matrix products, local(): jnp.dot(normed, w_single[side], preferred_element_type=jnp.float32)  3.18 us
    dot_general x1, matrix products, local(): jnp.dot(normed, w_query, preferred_element_type=jnp.float32)  2.93 us
    broadcast_in_dim x3, local copies, waits for them, and re-layouts, spread(): return exchange(jnp.broadcast_to(block[None], (peers,) + block.shape))  2.86 us
  transfers between devices with their start and end apart: 5, of which 5 were waited for; matrix products, arithmetic and copies ran while one was open for 9% of the time, Pallas kernels for 0%

profile of v1, /device:TPU:0, one launch (start us, length us, event | category | flops | bytes accessed | tf_op | source)
XLA Modules:
  0.0 88.8 jit_solution(18402851654888204063)
XLA Ops:
  0.6 1.5 %broadcast_in_dim.24 = bf16[8,24,512]{2,1,0:T(8,128)(2,1)} broadcast(bf16[24,512]{1,0:T(8,128)(2,1)} %param.21), dimensions={1,2} | broadcast | bytes 221184 | tf_op jit(solution)/shard_map/broadcast_in_dim | solution.py:26
  2.1 7.3 %all-to-all-start = ((bf16[8,24,512]{2,1,0:T(8,128)(2,1)}), bf16[8,24,512]{2,1,0:T(8,128)(2,1)S(1)}, u32[]{:S(2)}, u32[]{:S(2)}) async-start(bf16[8,24,512]{2,1,0:T(8,128)(2,1)} %broadcast_in_dim.24), calls=%async_computation | async-start | bytes 393216 | tf_op jit(solution)/shard_map/all_to_all | solution.py:21
  9.4 0.7 mul.240
  10.1 0.7 iota_compare_fusion
  10.9 6.5 %all-to-all-done = bf16[8,24,512]{2,1,0:T(8,128)(2,1)S(1)} async-done(((bf16[8,24,512]{2,1,0:T(8,128)(2,1)}), bf16[8,24,512]{2,1,0:T(8,128)(2,1)S(1)}, u32[]{:S(2)}, u32[]{:S(2)}) %all-to-all-start) | async-done | bytes 196640 | tf_op jit(solution)/shard_map/all_to_all | solution.py:21
  17.6 2.9 %convolution_convert_fusion.2 = bf16[24,512]{1,0:T(8,128)(2,1)S(1)} fusion(bf16[4096,512]{1,0:T(8,128)(2,1)} %param.23, f32[24,4096]{1,0:T(8,128)S(1)} %bitcast.120, f32[4096]{0:T(1024)} %param.22, f32[24]{0:T(128)S(1)} %add_rsqrt_fusion.1), kind=kOutput, calls=%fused_computation.15 | convolution fusion | flops 100970496 | bytes 4628576 | tf_op jit(solution)/shard_map/dot_general | solution.py:119
  20.7 1.7 %fusion.44 = (f32[24,128]{1,0:T(8,128)S(1)}, bf16[24,128]{1,0:T(8,128)(2,1)S(1)}) fusion(bf16[24,4096]{1,0:T(8,128)(2,1)S(1)} %bitcast.118, bf16[2,4096,512]{2,1,0:T(8,128)(2,1)} %param.24), kind=kOutput, calls=%fused_computation.92 | convolution fusion | flops 25171968 | bytes 1263616 | tf_op jit(solution)/shard_map/dot_general | solution.py:130
  22.5 1.5 %fusion.46 = (f32[24,128]{1,0:T(8,128)S(1)}, bf16[24,128]{1,0:T(8,128)(2,1)S(1)}) fusion(bf16[24,4096]{1,0:T(8,128)(2,1)S(1)} %bitcast.119, bf16[2,4096,512]{2,1,0:T(8,128)(2,1)} %param.24), kind=kOutput, calls=%fused_computation.94 | convolution fusion | flops 25171968 | bytes 1263616 | tf_op jit(solution)/shard_map/dot_general | solution.py:130
  24.1 1.8 %fusion.45 = (f32[24,4]{1,0:T(8,128)S(1)}, f32[24,4,128]{2,1,0:T(4,128)S(1)}) fusion(bf16[24,4,128]{2,1,0:T(4,128)(2,1)S(1)} %reshape.306, bf16[2,24,4,128,128]{4,3,2,1,0:T(8,128)(2,1)} %param.26, pred[24,128]{1,0:T(8,128)(4,1)S(1)} %iota_compare_fusion), kind=kOutput, calls=%fused_computation.93 | convolution fusion | flops 3182496 | bytes 863616 | tf_op jit(solution)/shard_map/bgqd,bgtd->bgqt/dot_general | solution.py:53
  26.1 1.5 %fusion.7 = bf16[24,4,128]{2,1,0:T(4,128)(2,1)S(1)} fusion(bf16[2,24,4,128,128]{4,3,2,1,0:T(8,128)(2,1)} %param.26, f32[24,4,128]{2,1,0:T(4,128)S(1)} %get-tuple-element.22, f32[24,128]{1,0:T(8,128)S(1)} %get-tuple-element.19, f32[24,4]{1,0:T(8,128)S(1)} %get-tuple-element.12, f32[24,4]{1,0:T(8,128)S(1)} %get-tuple-element.11, ...), kind=kOutput, calls=%fused_computation.14 | convolution fusion | flops 3219456 | bytes 873600 | tf_op jit(solution)/shard_map/bgqt,bgtd->bgqd/dot_general | solution.py:70
  27.6 0.7 convolution_convert_fusion.1
  28.3 0.7 copy.77
  29.0 3.4 %all-to-all-start.1 = ((bf16[8,24,512]{2,1,0:T(8,128)(2,1)}), bf16[8,24,512]{2,1,0:T(8,128)(2,1)S(1)}, u32[]{:S(2)}, u32[]{:S(2)}) async-start(bf16[8,24,512]{2,1,0:T(8,128)(2,1)} %bitcast.117), calls=%async_computation.1 | async-start | bytes 393216 | tf_op jit(solution)/shard_map/all_to_all | solution.py:21
  32.8 7.4 %all-to-all-done.1 = bf16[8,24,512]{2,1,0:T(8,128)(2,1)S(1)} async-done(((bf16[8,24,512]{2,1,0:T(8,128)(2,1)}), bf16[8,24,512]{2,1,0:T(8,128)(2,1)S(1)}, u32[]{:S(2)}, u32[]{:S(2)}) %all-to-all-start.1) | async-done | bytes 196640 | tf_op jit(solution)/shard_map/all_to_all | solution.py:21
  40.2 0.7 broadcast_in_dim.26
  40.9 3.4 %all-to-all-start.2 = ((bf16[8,24,512]{2,1,0:T(8,128)(2,1)}), bf16[8,24,512]{2,1,0:T(8,128)(2,1)S(1)}, u32[]{:S(2)}, u32[]{:S(2)}) async-start(bf16[8,24,512]{2,1,0:T(8,128)(2,1)} %broadcast_in_dim.26), calls=%async_computation.2 | async-start | bytes 393216 | tf_op jit(solution)/shard_map/all_to_all | solution.py:21
  44.4 7.6 %all-to-all-done.2 = bf16[8,24,512]{2,1,0:T(8,128)(2,1)S(1)} async-done(((bf16[8,24,512]{2,1,0:T(8,128)(2,1)}), bf16[8,24,512]{2,1,0:T(8,128)(2,1)S(1)}, u32[]{:S(2)}, u32[]{:S(2)}) %all-to-all-start.2) | async-done | bytes 196640 | tf_op jit(solution)/shard_map/all_to_all | solution.py:21
  52.3 4.6 %fusion.41 = (f32[24,1024]{1,0:T(8,128)S(1)}, bf16[24,1024]{1,0:T(8,128)(2,1)S(1)}, f32[24,1024]{1,0:T(8,128)S(1)}) fusion(f32[1024]{0:T(1024)S(1)} %bitcast.131, f32[24,3,1024]{2,0,1:T(8,128)S(1)} %copy-done.3, f32[1024]{0:T(1024)S(1)} %bitcast.132, f32[1024]{0:T(1024)S(1)} %bitcast.130, f32[1024]{0:T(1024)S(1)} %bitcast.129, f32[1024]{0:T(1024)S(1)} %copy-done.14, ...), kind=kOutput, calls=%fused_computation.89 | convolution fusion | flops 201670656 | bytes 9146368 | tf_op jit(solution)/shard_map/dot_general | solution.py:144
  57.0 0.3 convolution_convert_fusion.3
  57.3 0.7 broadcast_in_dim.28
  58.0 3.4 %all-to-all-start.3 = ((bf16[8,24,291]{2,1,0:T(8,128)(2,1)}), bf16[8,24,291]{2,1,0:T(8,128)(2,1)S(1)}, u32[]{:S(2)}, u32[]{:S(2)}) async-start(bf16[8,24,291]{2,1,0:T(8,128)(2,1)} %broadcast_in_dim.28), calls=%async_computation.3 | async-start | bytes 294912 | tf_op jit(solution)/shard_map/all_to_all | solution.py:21
  61.4 4.8 %divide_multiply_fusion = f32[24,1024]{1,0:T(8,128)S(1)} fusion(bf16[24,4096]{1,0:T(8,128)(2,1)S(1)} %bitcast.124, bf16[2,4096,1024]{2,1,0:T(8,128)(2,1)} %param.29), kind=kOutput, calls=%fused_computation.57 | convolution fusion | flops 201424896 | bytes 8683520 | tf_op jit(solution)/shard_map/dot_general | solution.py:145
  66.2 2.6 %all-to-all-done.3 = bf16[8,24,291]{2,1,0:T(8,128)(2,1)S(1)} async-done(((bf16[8,24,291]{2,1,0:T(8,128)(2,1)}), bf16[8,24,291]{2,1,0:T(8,128)(2,1)S(1)}, u32[]{:S(2)}, u32[]{:S(2)}) %all-to-all-start.3) | async-done | bytes 111776 | tf_op jit(solution)/shard_map/all_to_all | solution.py:21
  69.2 2.0 %multiply_reduce_fusion = (f32[24,1024]{1,0:T(8,128)S(1)}, f32[24,16,1024]{2,1,0:T(8,128)}) fusion(f32[24,16]{1,0:T(8,128)S(1)} %get-tuple-element.10, f32[24,1024]{1,0:T(8,128)S(1)} %get-tuple-element.7, f32[24,16]{1,0:T(8,128)S(1)} %get-tuple-element.9, f32[24,1024]{1,0:T(8,128)S(1)} %get-tuple-element.27, f32[24,16,1024]{2,1,0:T(8,128)S(1)} %copy-done.2, ...), kind=kLoop, calls=%fused_computation.8 | loop fusion | flops 2727936 | bytes 3607552 | tf_op jit(solution)/shard_map/reduce_sum | solution.py:173
  71.1 4.6 %convolution_convert_fusion = bf16[24,4096]{1,0:T(8,128)(2,1)S(1)} fusion(bf16[1024,4096]{1,0:T(8,128)(2,1)} %param.39, f32[24,1024]{1,0:T(8,128)S(1)} %divide_multiply_fusion, f32[24,1024]{1,0:T(8,128)S(1)} %get-tuple-element.5, f32[1024]{0:T(1024)S(1)} %copy-done.6, bf16[24,1024]{1,0:T(8,128)(2,1)S(1)} %get-tuple-element.8), kind=kOutput, calls=%fused_computation.6 | convolution fusion | flops 201547776 | bytes 8835072 | tf_op jit(solution)/shard_map/dot_general | solution.py:176
  75.7 0.7 copy.76
  76.4 3.4 %all-to-all-start.4 = ((bf16[8,24,512]{2,1,0:T(8,128)(2,1)}), bf16[8,24,512]{2,1,0:T(8,128)(2,1)S(1)}, u32[]{:S(2)}, u32[]{:S(2)}) async-start(bf16[8,24,512]{2,1,0:T(8,128)(2,1)} %bitcast.115), calls=%async_computation.4 | async-start | bytes 393216 | tf_op jit(solution)/shard_map/all_to_all | solution.py:21
  79.9 0.7 pad_maximum_fusion
  80.6 0.7 slice_reduce_fusion
  81.3 6.3 %all-to-all-done.4 = bf16[8,24,512]{2,1,0:T(8,128)(2,1)S(1)} async-done(((bf16[8,24,512]{2,1,0:T(8,128)(2,1)}), bf16[8,24,512]{2,1,0:T(8,128)(2,1)S(1)}, u32[]{:S(2)}, u32[]{:S(2)}) %all-to-all-start.4) | async-done | bytes 196640 | tf_op jit(solution)/shard_map/all_to_all | solution.py:21
  87.6 0.6 add_convert_fusion
  88.2 0.6 reshape.312
  (66 shorter events, 2.0 us)
Async XLA Ops:
  0.6 56.3 %copy-start = (bf16[1024,288]{0,1:T(8,128)(2,1)S(1)}, bf16[1024,288]{0,1:T(8,128)(2,1)}, u32[]{:S(2)}) copy-start(bf16[1024,288]{0,1:T(8,128)(2,1)} %param.33) | copy-start | bytes 1769476
  2.1 15.2 %all-to-all-start = ((bf16[8,24,512]{2,1,0:T(8,128)(2,1)}), bf16[8,24,512]{2,1,0:T(8,128)(2,1)S(1)}, u32[]{:S(2)}, u32[]{:S(2)}) async-start(bf16[8,24,512]{2,1,0:T(8,128)(2,1)} %broadcast_in_dim.24), calls=%async_computation | async-start | bytes 393216 | tf_op jit(solution)/shard_map/all_to_all | solution.py:21
  20.6 7.0 %copy-start.1 = (bf16[512,4096]{1,0:T(8,128)(2,1)S(1)}, bf16[512,4096]{1,0:T(8,128)(2,1)}, u32[]{:S(2)}) copy-start(bf16[512,4096]{1,0:T(8,128)(2,1)} %param.25) | copy-start | bytes 12582916
  22.4 10.0 %copy-start.8 = (f32[4096]{0:T(1024)S(1)}, f32[4096]{0:T(1024)}, u32[]{:S(2)}) copy-start(f32[4096]{0:T(1024)} %param.28) | copy-start | bytes 49156
  22.4 10.0 %copy-start.10 = (f32[24,16]{0,1:T(8,128)S(1)}, f32[24,16]{0,1:T(8,128)}, u32[]{:S(2)}) copy-start(f32[24,16]{0,1:T(8,128)} %param.40) | copy-start | bytes 4612
  22.4 10.0 %copy-start.11 = (s32[24,16]{0,1:T(8,128)S(1)}, s32[24,16]{0,1:T(8,128)}, u32[]{:S(2)}) copy-start(s32[24,16]{0,1:T(8,128)} %param.41) | copy-start | bytes 4612
  22.4 10.0 %copy-start.13 = (s32[24]{0:T(128)S(1)}, s32[24]{0:T(128)}, u32[]{:S(2)}) copy-start(s32[24]{0:T(128)} %param.27) | copy-start | bytes 292
  24.0 16.2 %copy-start.5 = (bf16[24,512]{1,0:T(8,128)(2,1)S(1)}, bf16[24,512]{1,0:T(8,128)(2,1)}, u32[]{:S(2)}) copy-start(bf16[24,512]{1,0:T(8,128)(2,1)} %param.21) | copy-start | bytes 73732
  24.1 20.3 %copy-start.7 = (f32[16,1024]{1,0:T(8,128)S(1)}, f32[16,1024]{1,0:T(8,128)}, u32[]{:S(2)}) copy-start(f32[16,1024]{1,0:T(8,128)} %param.36) | copy-start | bytes 196612
  25.9 18.5 %copy-start.9 = (f32[4,1024]{1,0:T(4,128)S(1)}, f32[4,1024]{1,0:T(4,128)}, u32[]{:S(2)}) copy-start(f32[4,1024]{1,0:T(4,128)} %param.30) | copy-start | bytes 49156
  27.6 24.7 %copy-start.3 = (f32[24,3,1024]{2,0,1:T(8,128)S(1)}, f32[24,3,1024]{2,0,1:T(8,128)}, u32[]{:S(2)}) copy-start(f32[24,3,1024]{2,0,1:T(8,128)} %param.32) | copy-start | bytes 884740
  27.6 24.7 %copy-start.14 = (f32[1024]{0:T(1024)S(1)}, f32[1024]{0:T(1024)}, u32[]{:S(2)}) copy-start(f32[1024]{0:T(1024)} %param.31) | copy-start | bytes 12292
  29.0 11.1 %all-to-all-start.1 = ((bf16[8,24,512]{2,1,0:T(8,128)(2,1)}), bf16[8,24,512]{2,1,0:T(8,128)(2,1)S(1)}, u32[]{:S(2)}, u32[]{:S(2)}) async-start(bf16[8,24,512]{2,1,0:T(8,128)(2,1)} %bitcast.117), calls=%async_computation.1 | async-start | bytes 393216 | tf_op jit(solution)/shard_map/all_to_all | solution.py:21
  40.9 11.1 %all-to-all-start.2 = ((bf16[8,24,512]{2,1,0:T(8,128)(2,1)}), bf16[8,24,512]{2,1,0:T(8,128)(2,1)S(1)}, u32[]{:S(2)}, u32[]{:S(2)}) async-start(bf16[8,24,512]{2,1,0:T(8,128)(2,1)} %broadcast_in_dim.26), calls=%async_computation.2 | async-start | bytes 393216 | tf_op jit(solution)/shard_map/all_to_all | solution.py:21
  58.0 10.8 %all-to-all-start.3 = ((bf16[8,24,291]{2,1,0:T(8,128)(2,1)}), bf16[8,24,291]{2,1,0:T(8,128)(2,1)S(1)}, u32[]{:S(2)}, u32[]{:S(2)}) async-start(bf16[8,24,291]{2,1,0:T(8,128)(2,1)} %broadcast_in_dim.28), calls=%async_computation.3 | async-start | bytes 294912 | tf_op jit(solution)/shard_map/all_to_all | solution.py:21
  61.4 7.5 %copy-start.4 = (bf16[256,1024]{1,0:T(8,128)(2,1)S(1)}, bf16[256,1024]{1,0:T(8,128)(2,1)}, u32[]{:S(2)}) copy-start(bf16[256,1024]{1,0:T(8,128)(2,1)} %param.34) | copy-start | bytes 1572868
  61.4 7.5 %copy-start.12 = (f32[1024]{0:T(1024)S(1)}, f32[1024]{0:T(1024)}, u32[]{:S(2)}) copy-start(f32[1024]{0:T(1024)} %param.35) | copy-start | bytes 12292
  61.4 7.7 %copy-start.2 = (f32[24,16,1024]{2,1,0:T(8,128)S(1)}, f32[24,16,1024]{2,1,0:T(8,128)}, u32[]{:S(2)}) copy-start(f32[24,16,1024]{2,1,0:T(8,128)} %param.38) | copy-start | bytes 4718596
  66.2 4.9 %copy-start.6 = (f32[1024]{0:T(1024)S(1)}, f32[1024]{0:T(1024)}, u32[]{:S(2)}) copy-start(f32[1024]{0:T(1024)} %param.37) | copy-start | bytes 12292
  71.1 8.7 %slice-start = ((f32[24,3,1024]{2,0,1:T(8,128)}), f32[24,2,1024]{2,0,1:T(8,128)S(1)}, s32[]{:S(2)}) async-start(f32[24,3,1024]{2,0,1:T(8,128)} %param.32), calls=%async_computation.5 | async-start | bytes 393216 | tf_op jit(solution)/shard_map/slice | solution.py:152
  76.4 11.1 %all-to-all-start.4 = ((bf16[8,24,512]{2,1,0:T(8,128)(2,1)}), bf16[8,24,512]{2,1,0:T(8,128)(2,1)S(1)}, u32[]{:S(2)}, u32[]{:S(2)}) async-start(bf16[8,24,512]{2,1,0:T(8,128)(2,1)} %bitcast.115), calls=%async_computation.4 | async-start | bytes 393216 | tf_op jit(solution)/shard_map/all_to_all | solution.py:21
